TPU v7x, 32 devices: a whole 2x2x4 slice. The times are simulated.
32 devices in a mesh: dp: 8 (over z, x), ctx: 4 (over y, core).
Axes of the slice: x: 2, y: 2, z: 4, core: 2. Of those that a mesh axis runs over, the one named last changes fastest.
Arguments:
- inputs: bfloat16 [8, 2048, 768], P('dp', 'ctx'), may hold values from -6 to 6
- segments: int32 [8, 2048], P('dp'), may hold values from 0 to 34, as said below
- qkv_weight: bfloat16 [768, 2304], P(('dp', 'ctx')), may hold values from -0.21875 to 0.21875
- query_value_bias: bfloat16 [1536], P(('dp', 'ctx')), may hold values from -3 to 3
- output_weight: bfloat16 [768, 768], P(('dp', 'ctx')), may hold values from -1.75 to 1.75
- output_bias: bfloat16 [768], P(('dp', 'ctx')), may hold values from -3 to 3
- attention_gain: bfloat16 [768], P(('dp', 'ctx')), may hold values from 0.25 to 1.75
- attention_shift: bfloat16 [768], P(('dp', 'ctx')), may hold values from -2 to 2
- up_weight: bfloat16 [768, 3072], P(('dp', 'ctx')), may hold values from -0.21875 to 0.21875
- up_bias: bfloat16 [3072], P(('dp', 'ctx')), may hold values from -3 to 3
- down_weight: bfloat16 [3072, 768], P(('dp', 'ctx')), may hold values from -0.109375 to 0.109375
- down_bias: bfloat16 [768], P(('dp', 'ctx')), may hold values from -3 to 3
- final_gain: bfloat16 [768], P(('dp', 'ctx')), may hold values from 0.25 to 1.75
- final_shift: bfloat16 [768], P(('dp', 'ctx')), may hold values from -2 to 2
- cotangent: bfloat16 [8, 2048, 768], P('dp', 'ctx'), may hold values from -6 to 6
Outputs:
- output: bfloat16 [8, 2048, 768], P('dp', 'ctx')
- input_grad: float32 [8, 2048, 768], P('dp', 'ctx')
- qkv_weight_grad: float32 [768, 2304], P(('dp', 'ctx'))
- query_value_bias_grad: float32 [1536], P(('dp', 'ctx'))
- output_weight_grad: float32 [768, 768], P(('dp', 'ctx'))
- output_bias_grad: float32 [768], P(('dp', 'ctx'))
- attention_gain_grad: float32 [768], P(('dp', 'ctx'))
- attention_shift_grad: float32 [768], P(('dp', 'ctx'))
- up_weight_grad: float32 [768, 3072], P(('dp', 'ctx'))
- up_bias_grad: float32 [3072], P(('dp', 'ctx'))
- down_weight_grad: float32 [3072, 768], P(('dp', 'ctx'))
- down_bias_grad: float32 [768], P(('dp', 'ctx'))
- final_gain_grad: float32 [768], P(('dp', 'ctx'))
- final_shift_grad: float32 [768], P(('dp', 'ctx'))
Inputs may be any that keep to these rules, and one draw needn't show every extreme that they name: `segments`: in each sequence, segment numbers count its whole documents from 1 in order of position; each document spans 60 to 800 positions; the positions after the last whole document, one or more, are 0. The first sequence is packed with documents of exactly 60 positions.
All inputs are finite; a program needn't handle non-finite values.
Results may differ from a plain program's by a relative error of at most 0.017.
Values may be sent and summed in bfloat16 or wider, within the bound.
No kernel may reach another device: no remote copies, remote signals or barrier semaphores. Data moves between devices by JAX's collectives and lax.ppermute only.
A program may use at most 128 MiB of HBM per device.

v0:
```python
import jax
import jax.numpy as jnp
from jax import lax
from jax.sharding import PartitionSpec as P

HEADS = 12
HEAD_DIM = 64
MASKED = -1000000000.0


def layer_norm(rows, gain, shift):
    center = jnp.mean(rows, axis=-1, keepdims=True)
    centred = rows - center
    spread = jnp.mean(centred * centred, axis=-1, keepdims=True)
    return centred * lax.rsqrt(spread + 1e-06) * gain + shift


def exact_gelu(values):
    return jax.nn.gelu(values, approximate=False)


def inner_rows(left, right):
    return lax.dot_general(
        left, right, (((0,), (0,)), ((), ())), preferred_element_type=jnp.float32
    )


def times_transpose(left, right):
    return lax.dot_general(
        left, right, (((1,), (1,)), ((), ())), preferred_element_type=jnp.float32
    )


def shards(
    inputs,
    segments,
    qkv_weight,
    query_value_bias,
    output_weight,
    output_bias,
    attention_gain,
    attention_shift,
    up_weight,
    up_bias,
    down_weight,
    down_bias,
    final_gain,
    final_shift,
    cotangent,
):
    gathered = (
        lax.all_gather(qkv_weight, ("dp", "ctx"), axis=0, tiled=True),
        lax.all_gather(query_value_bias, ("dp", "ctx"), axis=0, tiled=True),
        lax.all_gather(output_weight, ("dp", "ctx"), axis=0, tiled=True),
        lax.all_gather(output_bias, ("dp", "ctx"), axis=0, tiled=True),
        lax.all_gather(attention_gain, ("dp", "ctx"), axis=0, tiled=True),
        lax.all_gather(attention_shift, ("dp", "ctx"), axis=0, tiled=True),
        lax.all_gather(up_weight, ("dp", "ctx"), axis=0, tiled=True),
        lax.all_gather(up_bias, ("dp", "ctx"), axis=0, tiled=True),
        lax.all_gather(down_weight, ("dp", "ctx"), axis=0, tiled=True),
        lax.all_gather(down_bias, ("dp", "ctx"), axis=0, tiled=True),
        lax.all_gather(final_gain, ("dp", "ctx"), axis=0, tiled=True),
        lax.all_gather(final_shift, ("dp", "ctx"), axis=0, tiled=True),
    )
    (
        qkv_full,
        bias_qv,
        out_full,
        bias_out,
        gain_one,
        shift_one,
        up_full,
        bias_up,
        down_full,
        bias_down,
        gain_two,
        shift_two,
    ) = gathered
    seq_count, group, width = inputs.shape
    row_total = seq_count * group
    seq_len = group * lax.axis_size("ctx")
    flat_in = inputs.reshape(row_total, width)
    zero_keys = jnp.zeros((width,), jnp.float32)
    bias_f32 = bias_qv.astype(jnp.float32)
    qkv_bias = jnp.concatenate([bias_f32[:width], zero_keys, bias_f32[width:]])
    qkv_rows = jnp.dot(flat_in, qkv_full, preferred_element_type=jnp.float32) + qkv_bias
    queries = (
        (qkv_rows[:, :width] * 0.125)
        .astype(jnp.bfloat16)
        .reshape(seq_count, group, HEADS, HEAD_DIM)
    )
    key_rows = qkv_rows[:, width : 2 * width].astype(jnp.bfloat16).reshape(seq_count, group, width)
    value_rows = qkv_rows[:, 2 * width :].astype(jnp.bfloat16).reshape(seq_count, group, width)
    offset = lax.axis_index("ctx") * group
    query_seg = lax.dynamic_slice_in_dim(segments, offset, group, 1)

    def allowed_mask(key_seg):
        return (query_seg[:, :, None, None] == key_seg[:, None, None, :]) & (
            key_seg[:, None, None, :] > 0
        )

    def block_pieces(piece_keys, piece_values, begin, block_size):
        block_keys = lax.dynamic_slice_in_dim(piece_keys, begin, block_size, 1).reshape(
            seq_count, block_size, HEADS, HEAD_DIM
        )
        block_values = lax.dynamic_slice_in_dim(piece_values, begin, block_size, 1).reshape(
            seq_count, block_size, HEADS, HEAD_DIM
        )
        key_seg = lax.dynamic_slice_in_dim(segments, begin, block_size, 1)
        scores = jnp.einsum(
            "bqhd,bkhd->bqhk", queries, block_keys, preferred_element_type=jnp.float32
        )
        masked = jnp.where(allowed_mask(key_seg), scores, MASKED)
        return (block_keys, block_values, masked)

    start_state = (
        jnp.zeros((seq_count, group, HEADS, HEAD_DIM), jnp.float32),
        jnp.zeros((seq_count, group, HEADS), jnp.float32),
        jnp.zeros((seq_count, group, HEADS), jnp.float32),
    )
    piece_keys = lax.all_gather(key_rows, "ctx", axis=1, tiled=True)
    piece_values = lax.all_gather(value_rows, "ctx", axis=1, tiled=True)
    span = piece_keys.shape[1]
    block_size = 512

    def forward_one_block(state, block_index):
        running, row_max, row_sum = state
        begin = block_index * block_size
        block_keys, block_values, masked = block_pieces(piece_keys, piece_values, begin, block_size)
        new_max = jnp.maximum(row_max, jnp.max(masked, axis=-1))
        rescale = jnp.exp(row_max - new_max)
        weights = jnp.exp(masked - new_max[..., None])
        row_sum = row_sum * rescale + jnp.sum(weights, axis=-1)
        running = running * rescale[..., None] + jnp.einsum(
            "bqhk,bkhd->bqhd",
            weights.astype(jnp.bfloat16),
            block_values,
            preferred_element_type=jnp.float32,
        )
        return ((running, new_max, row_sum), None)

    state, unused = lax.scan(
        forward_one_block, start_state, jnp.arange(span // block_size, dtype=jnp.int32)
    )
    running, row_max, row_sum = state
    safe_sum = jnp.where(query_seg[:, :, None] > 0, row_sum, 1.0)
    attended = running / safe_sum[..., None]
    mixed_low = attended.reshape(row_total, width).astype(jnp.bfloat16)
    resid_one = (
        flat_in.astype(jnp.float32)
        + jnp.dot(mixed_low, out_full, preferred_element_type=jnp.float32)
        + bias_out.astype(jnp.float32)
    )
    normed, first_back = jax.vjp(
        layer_norm, resid_one, gain_one.astype(jnp.float32), shift_one.astype(jnp.float32)
    )
    normed_low = normed.astype(jnp.bfloat16)
    hidden_pre = jnp.dot(normed_low, up_full, preferred_element_type=jnp.float32) + bias_up.astype(
        jnp.float32
    )
    hidden_low = exact_gelu(hidden_pre).astype(jnp.bfloat16)
    resid_two = (
        normed
        + jnp.dot(hidden_low, down_full, preferred_element_type=jnp.float32)
        + bias_down.astype(jnp.float32)
    )
    result, final_back = jax.vjp(
        layer_norm, resid_two, gain_two.astype(jnp.float32), shift_two.astype(jnp.float32)
    )
    output = result.astype(jnp.bfloat16).reshape(seq_count, group, width)
    regathered = (
        lax.all_gather(qkv_weight, ("dp", "ctx"), axis=0, tiled=True),
        lax.all_gather(query_value_bias, ("dp", "ctx"), axis=0, tiled=True),
        lax.all_gather(output_weight, ("dp", "ctx"), axis=0, tiled=True),
        lax.all_gather(output_bias, ("dp", "ctx"), axis=0, tiled=True),
        lax.all_gather(attention_gain, ("dp", "ctx"), axis=0, tiled=True),
        lax.all_gather(attention_shift, ("dp", "ctx"), axis=0, tiled=True),
        lax.all_gather(up_weight, ("dp", "ctx"), axis=0, tiled=True),
        lax.all_gather(up_bias, ("dp", "ctx"), axis=0, tiled=True),
        lax.all_gather(down_weight, ("dp", "ctx"), axis=0, tiled=True),
        lax.all_gather(down_bias, ("dp", "ctx"), axis=0, tiled=True),
        lax.all_gather(final_gain, ("dp", "ctx"), axis=0, tiled=True),
        lax.all_gather(final_shift, ("dp", "ctx"), axis=0, tiled=True),
    )
    qkv_back = regathered[0]
    out_back = regathered[2]
    up_back = regathered[6]
    down_back = regathered[8]
    grad_out = cotangent.reshape(row_total, width).astype(jnp.float32)
    grad_resid_two, final_gain_grad, final_shift_grad = final_back(grad_out)
    grad_down_in = grad_resid_two.astype(jnp.bfloat16)
    down_bias_grad = jnp.sum(grad_down_in.astype(jnp.float32), axis=0)
    down_weight_grad = inner_rows(hidden_low, grad_down_in)
    grad_hidden = times_transpose(grad_down_in, down_back)
    unused_value, gelu_pull = jax.vjp(exact_gelu, hidden_pre)
    grad_pre = gelu_pull(grad_hidden)[0].astype(jnp.bfloat16)
    up_bias_grad = jnp.sum(grad_pre.astype(jnp.float32), axis=0)
    up_weight_grad = inner_rows(normed_low, grad_pre)
    grad_normed = grad_resid_two + times_transpose(grad_pre, up_back)
    grad_resid_one, attention_gain_grad, attention_shift_grad = first_back(grad_normed)
    grad_mix_in = grad_resid_one.astype(jnp.bfloat16)
    output_bias_grad = jnp.sum(grad_mix_in.astype(jnp.float32), axis=0)
    output_weight_grad = inner_rows(mixed_low, grad_mix_in)
    grad_mixed = (
        times_transpose(grad_mix_in, out_back)
        .astype(jnp.bfloat16)
        .reshape(seq_count, group, HEADS, HEAD_DIM)
    )
    delta_rows = jnp.sum(grad_mixed.astype(jnp.float32) * attended, axis=-1)
    back_state = (
        jnp.zeros((seq_count, group, HEADS, HEAD_DIM), jnp.float32),
        jnp.zeros((seq_count, seq_len, width), jnp.float32),
        jnp.zeros((seq_count, seq_len, width), jnp.float32),
    )
    backward_piece_keys = lax.all_gather(key_rows, "ctx", axis=1, tiled=True)
    backward_piece_values = lax.all_gather(value_rows, "ctx", axis=1, tiled=True)
    span = backward_piece_keys.shape[1]
    backward_block_size = 512

    def backward_one_block(state, block_index):
        grad_query, grad_keys, grad_values = state
        begin = block_index * backward_block_size
        block_keys, block_values, masked = block_pieces(
            backward_piece_keys, backward_piece_values, begin, backward_block_size
        )
        probs = jnp.exp(masked - row_max[..., None]) / safe_sum[..., None]
        grad_probs = jnp.einsum(
            "bqhd,bkhd->bqhk", grad_mixed, block_values, preferred_element_type=jnp.float32
        )
        grad_scores = (probs * (grad_probs - delta_rows[..., None])).astype(jnp.bfloat16)
        grad_query = grad_query + jnp.einsum(
            "bqhk,bkhd->bqhd", grad_scores, block_keys, preferred_element_type=jnp.float32
        )
        key_part = jnp.einsum(
            "bqhk,bqhd->bkhd", grad_scores, queries, preferred_element_type=jnp.float32
        ).reshape(seq_count, backward_block_size, width)
        value_part = jnp.einsum(
            "bqhk,bqhd->bkhd",
            probs.astype(jnp.bfloat16),
            grad_mixed,
            preferred_element_type=jnp.float32,
        ).reshape(seq_count, backward_block_size, width)
        grad_keys = lax.dynamic_update_slice_in_dim(grad_keys, key_part, begin, 1)
        grad_values = lax.dynamic_update_slice_in_dim(grad_values, value_part, begin, 1)
        return ((grad_query, grad_keys, grad_values), None)

    state, unused = lax.scan(
        backward_one_block, back_state, jnp.arange(span // backward_block_size, dtype=jnp.int32)
    )
    grad_query, grad_keys, grad_values = state
    own_keys, own_values = (
        lax.psum_scatter(
            grad_keys.astype(jnp.bfloat16), "ctx", scatter_dimension=1, tiled=True
        ).astype(jnp.float32),
        lax.psum_scatter(
            grad_values.astype(jnp.bfloat16), "ctx", scatter_dimension=1, tiled=True
        ).astype(jnp.float32),
    )
    grad_qkv = jnp.concatenate(
        [
            grad_query.reshape(row_total, width) * 0.125,
            own_keys.reshape(row_total, width),
            own_values.reshape(row_total, width),
        ],
        axis=1,
    ).astype(jnp.bfloat16)
    column_sums = jnp.sum(grad_qkv.astype(jnp.float32), axis=0)
    qv_bias_grad = jnp.concatenate([column_sums[:width], column_sums[2 * width :]])
    qkv_weight_grad = inner_rows(flat_in, grad_qkv)
    input_grad = (grad_resid_one + times_transpose(grad_qkv, qkv_back)).reshape(
        seq_count, group, width
    )
    shares = (
        lax.psum_scatter(qkv_weight_grad, ("dp", "ctx"), scatter_dimension=0, tiled=True),
        lax.psum_scatter(qv_bias_grad, ("dp", "ctx"), scatter_dimension=0, tiled=True),
        lax.psum_scatter(output_weight_grad, ("dp", "ctx"), scatter_dimension=0, tiled=True),
        lax.psum_scatter(output_bias_grad, ("dp", "ctx"), scatter_dimension=0, tiled=True),
        lax.psum_scatter(attention_gain_grad, ("dp", "ctx"), scatter_dimension=0, tiled=True),
        lax.psum_scatter(attention_shift_grad, ("dp", "ctx"), scatter_dimension=0, tiled=True),
        lax.psum_scatter(up_weight_grad, ("dp", "ctx"), scatter_dimension=0, tiled=True),
        lax.psum_scatter(up_bias_grad, ("dp", "ctx"), scatter_dimension=0, tiled=True),
        lax.psum_scatter(down_weight_grad, ("dp", "ctx"), scatter_dimension=0, tiled=True),
        lax.psum_scatter(down_bias_grad, ("dp", "ctx"), scatter_dimension=0, tiled=True),
        lax.psum_scatter(final_gain_grad, ("dp", "ctx"), scatter_dimension=0, tiled=True),
        lax.psum_scatter(final_shift_grad, ("dp", "ctx"), scatter_dimension=0, tiled=True),
    )
    return (
        output,
        input_grad,
        shares[0],
        shares[1],
        shares[2],
        shares[3],
        shares[4],
        shares[5],
        shares[6],
        shares[7],
        shares[8],
        shares[9],
        shares[10],
        shares[11],
    )


def solution(mesh):
    placed = (
        P("dp", "ctx", None),
        P("dp", None),
        P(("dp", "ctx"), None),
        P(("dp", "ctx")),
        P(("dp", "ctx"), None),
        P(("dp", "ctx")),
        P(("dp", "ctx")),
        P(("dp", "ctx")),
        P(("dp", "ctx"), None),
        P(("dp", "ctx")),
        P(("dp", "ctx"), None),
        P(("dp", "ctx")),
        P(("dp", "ctx")),
        P(("dp", "ctx")),
        P("dp", "ctx", None),
    )
    return jax.shard_map(
        shards,
        mesh=mesh,
        in_specs=placed,
        out_specs=(
            P("dp", "ctx", None),
            P("dp", "ctx", None),
            P(("dp", "ctx"), None),
            P(("dp", "ctx")),
            P(("dp", "ctx"), None),
            P(("dp", "ctx")),
            P(("dp", "ctx")),
            P(("dp", "ctx")),
            P(("dp", "ctx"), None),
            P(("dp", "ctx")),
            P(("dp", "ctx"), None),
            P(("dp", "ctx")),
            P(("dp", "ctx")),
            P(("dp", "ctx")),
        ),
        check_vma=False,
    )
```

profile of v0, /device:TPU:0, one launch (start us, length us, event | category | flops | bytes accessed | tf_op | source)
XLA Modules:
  0.0 1081.2 jit_solution(16484203945727431277)
XLA Ops:
  14.7 42.5 %all-reduce.17 = (bf16[1536]{0:T(1024)(128)(2,1)S(1)}, bf16[768]{0:T(1024)(128)(2,1)S(1)}, bf16[768]{0:T(1024)(128)(2,1)S(1)}, bf16[768]{0:T(1024)(128)(2,1)S(1)...) all-reduce(bf16[1536]{0:T(1024)(128)(2,1)S(1)} %dynamic-update-slic, ...), channel_id=1, replica_groups=mesh['dp'=8,'ctx'=4] {'dp','ctx'}, use_global_device_ids=true, to_apply=%add | all-reduce | flops 9216 | bytes 36864
  57.2 16.5 %all-gather.9.cloned.1.call-done = bf16[768,2304]{1,0:T(8,128)(2,1)} async-done(((bf16[24,2304]{1,0:T(8,128)(2,1)}), bf16[768,2304]{1,0:T(8,128)(2,1)}) %all-gather.9.cloned.1.call-update) | async-done | bytes 3538960 | tf_op jit(solution)/shard_map/all_gather | solution.py:52
  86.7 22.2 %all-gather.17.cloned.1.call-done = bf16[2048,768]{1,0:T(8,128)(2,1)} async-done(((bf16[512,768]{1,0:T(8,128)(2,1)}), bf16[2048,768]{1,0:T(8,128)(2,1)}) %all-gather.17.cloned.1.call-update) | async-done | bytes 3145744 | tf_op jit(solution)/shard_map/all_gather | solution.py:121
  113.6 26.0 %all-gather.19.cloned.1.call-done = bf16[2048,768]{1,0:T(8,128)(2,1)} async-done(((bf16[512,768]{1,0:T(8,128)(2,1)}), bf16[2048,768]{1,0:T(8,128)(2,1)}) %all-gather.19.cloned.1.call-update) | async-done | bytes 3145744 | tf_op jit(solution)/shard_map/all_gather | solution.py:122
  144.3 83.3 %while.30 = (s32[]{:T(128)}, f32[1,512,12,64]{1,3,2,0:T(8,128)S(1)}, f32[1,512,12]{1,2,0:T(8,128)S(1)}, f32[1,512,12]{1,2,0:T(8,128)S(1)}, s32[1,512]{1,0:T(1,12...) while((s32[]{:T(128)}, ...), condition=%wide.region_3.4_spmd.clone, body=%wide.region_0.3_spmd.clone.sunk | while | flops 832213504 | bytes 98184608 | solution.py:142
  153.8 6.9 fusion.118
  174.6 6.9 fusion.118
  195.4 6.9 fusion.118
  216.2 6.9 fusion.118
  232.7 28.9 %all-gather.13.cloned.1.call-done = bf16[768,3072]{1,0:T(8,128)(2,1)} async-done(((bf16[24,3072]{1,0:T(8,128)(2,1)}), bf16[768,3072]{1,0:T(8,128)(2,1)}) %all-gather.13.cloned.1.call-update) | async-done | bytes 4718608 | tf_op jit(solution)/shard_map/all_gather | solution.py:58
  261.6 21.0 %multiply_convert_fusion = (bf16[512,3072]{1,0:T(8,128)(2,1)}, f32[512,3072]{1,0:T(8,128)}, f32[512,3072]{1,0:T(8,128)}) fusion(f32[3072]{0:T(1024)S(1)} %convert_element_type.115, bf16[768,3072]{1,0:T(8,128)(2,1)} %all-gather.13.cloned.1.call-done, f32[512,768]{1,0:T(8,128)} %copy-done.11, f32[768]{0:T(1024)S(1)} %convert_element_type.113, ...), kind=kOutput, calls=%fused_computation.55 | convolution fusion | flops 2521694208 | bytes 22042624 | tf_op jit(solution)/shard_map/dot_general | solution.py:158
  282.6 43.6 %all-gather.15.cloned.1.call-done = bf16[3072,768]{1,0:T(8,128)(2,1)} async-done(((bf16[96,768]{1,0:T(8,128)(2,1)}), bf16[3072,768]{1,0:T(8,128)(2,1)}) %all-gather.15.cloned.1.call-update) | async-done | bytes 4718608 | tf_op jit(solution)/shard_map/all_gather | solution.py:60
  337.0 9.2 convert_reduce_fusion
  362.3 121.7 %while.31 = (s32[]{:T(128)}, f32[1,512,12,64]{1,3,2,0:T(8,128)}, bf16[1,2048,768]{1,2,0:T(8,128)(2,1)}, bf16[1,2048,768]{1,2,0:T(8,128)(2,1)}, s32[4]{0:T(128)S(...) while((s32[]{:T(128)}, f32[1,512,12,64]{1,3,2,0:T(8,128)}, ...), condition=%wide.region_14.15_spmd.clone, body=%wide.region_13.14_spmd.clone.sunk | while | flops 2046034432 | bytes 124390832 | solution.py:247
  487.8 7.3 fusion.52
  496.2 8.2 fusion.66
  506.0 14.3 %reduce-scatter.9.cloned.1.call-done = bf16[1,512,768]{1,2,0:T(8,128)(2,1)} async-done(((bf16[1,2048,768]{1,2,0:T(8,128)(2,1)}), bf16[1,512,768]{1,2,0:T(8,128)(2,1)}) %reduce-scatter.9.cloned.1.call-update) | async-done | bytes 786448 | tf_op jit(solution)/shard_map/reduce_scatter | solution.py:252
  520.3 40.3 %reduce-scatter.11.cloned.1.call-done = bf16[1,512,768]{1,2,0:T(8,128)(2,1)} async-done(((bf16[1,2048,768]{1,2,0:T(8,128)(2,1)}), bf16[1,512,768]{1,2,0:T(8,128)(2,1)}) %reduce-scatter.11.cloned.1.call-update) | async-done | bytes 786448 | tf_op jit(solution)/shard_map/reduce_scatter | solution.py:255
  566.8 8.0 copy.68
  577.9 40.2 %all-reduce.16 = (f32[1536]{0:T(1024)S(1)}, f32[768]{0:T(1024)S(1)}, f32[768]{0:T(1024)S(1)}, f32[768]{0:T(1024)S(1)}, f32[3072]{0:T(1024)S(1)}, /*index=5*/f32[...) all-reduce(f32[1536]{0:T(1024)S(1)} %pad_maximum_fusion.2, ...), channel_id=7, replica_groups=mesh['dp'=8,'ctx'=4] {'dp','ctx'}, use_global_device_ids=true, to_apply=%region_19.20.clone | all-reduce | flops 9216 | bytes 73728
  628.6 37.6 %reduce-scatter.13.cloned.1.call-done = f32[24,768]{1,0:T(8,128)} async-done(((f32[768,768]{1,0:T(8,128)}), f32[24,768]{1,0:T(8,128)}) %reduce-scatter.13.cloned.1.call-update) | async-done | bytes 73744 | tf_op jit(solution)/shard_map/reduce_scatter | solution.py:276
  666.2 141.6 %reduce-scatter.15.cloned.1.call-done = f32[24,3072]{1,0:T(8,128)} async-done(((f32[768,3072]{1,0:T(8,128)}), f32[24,3072]{1,0:T(8,128)}) %reduce-scatter.15.cloned.1.call-update) | async-done | bytes 294928 | tf_op jit(solution)/shard_map/reduce_scatter | solution.py:280
  807.8 141.7 %reduce-scatter.17.cloned.1.call-done = f32[96,768]{1,0:T(8,128)} async-done(((f32[3072,768]{1,0:T(8,128)}), f32[96,768]{1,0:T(8,128)}) %reduce-scatter.17.cloned.1.call-update) | async-done | bytes 294928 | tf_op jit(solution)/shard_map/reduce_scatter | solution.py:282
  949.5 124.7 %reduce-scatter.19.cloned.1.call-done = f32[24,2304]{1,0:T(8,128)} async-done(((f32[768,2304]{1,0:T(8,128)}), f32[24,2304]{1,0:T(8,128)}) %reduce-scatter.19.cloned.1.call-update) | async-done | bytes 221200
  (351 shorter events, 258.9 us)
Async XLA Ops:
  7.2 66.6 %all-gather.9.cloned.1.call-start = ((), (), s32[]{:S(2)}) async-start(), calls=%async_computation.6 | async-start | bytes 3649536 | tf_op jit(solution)/shard_map/all_gather | solution.py:52
  7.9 100.9 %all-gather.17.cloned.1.call-start = ((), (), s32[]{:S(2)}) async-start(), calls=%async_computation.15 | async-start | bytes 3932160 | tf_op jit(solution)/shard_map/all_gather | solution.py:121
  81.4 58.1 %all-gather.19.cloned.1.call-start = ((), (), s32[]{:S(2)}) async-start(), calls=%async_computation.16 | async-start | bytes 3932160 | tf_op jit(solution)/shard_map/all_gather | solution.py:122
  82.1 145.7 %all-gather.11.cloned.1.call-start = ((), (), s32[]{:S(2)}) async-start(), calls=%async_computation.7 | async-start | bytes 1216512 | tf_op jit(solution)/shard_map/all_gather | solution.py:54
  82.7 178.9 %all-gather.13.cloned.1.call-start = ((), (), s32[]{:S(2)}) async-start(), calls=%async_computation.8 | async-start | bytes 4866048 | tf_op jit(solution)/shard_map/all_gather | solution.py:58
  83.3 242.9 %all-gather.15.cloned.1.call-start = ((), (), s32[]{:S(2)}) async-start(), calls=%async_computation.9 | async-start | bytes 4866048 | tf_op jit(solution)/shard_map/all_gather | solution.py:60
  83.9 436.4 %reduce-scatter.9.cloned.1.call-start = ((), (), s32[]{:S(2)}) async-start(), calls=%async_computation.10 | async-start | bytes 3932160 | tf_op jit(solution)/shard_map/reduce_scatter | solution.py:252
  84.7 265.2 %copy-start.29 = (f32[768]{0:T(1024)}, f32[768]{0:T(1024)S(1)}, u32[]{:S(2)}) copy-start(f32[768]{0:T(1024)S(1)} %convert_element_type.112) | copy-start | bytes 9220
  84.8 241.5 %copy-start.36 = (f32[768]{0:T(1024)}, f32[768]{0:T(1024)S(1)}, u32[]{:S(2)}) copy-start(f32[768]{0:T(1024)S(1)} %convert_element_type.113) | copy-start | bytes 9220
  216.2 8.3 copy-start
  230.6 119.3 %copy-start.24 = (f32[512]{0:T(512)}, f32[512]{0:T(512)S(1)}, u32[]{:S(2)}) copy-start(f32[512]{0:T(512)S(1)} %broadcast_multiply_fusion.1) | copy-start | bytes 6148
  232.0 117.9 %copy-start.32 = (f32[512]{0:T(512)}, f32[512]{0:T(512)S(1)}, u32[]{:S(2)}) copy-start(f32[512]{0:T(512)S(1)} %fusion.50) | copy-start | bytes 6148
  336.0 10.2 slice-start
  336.8 9.4 copy-start.20
  337.0 9.2 copy-start.12
  337.0 9.2 slice-start.1
  484.1 76.5 %reduce-scatter.11.cloned.1.call-start = ((), (), s32[]{:S(2)}) async-start(), calls=%async_computation.11 | async-start | bytes 3932160 | tf_op jit(solution)/shard_map/reduce_scatter | solution.py:255
  484.9 181.3 %reduce-scatter.13.cloned.1.call-start = ((), (), s32[]{:S(2)}) async-start(), calls=%async_computation.12 | async-start | bytes 2433024 | tf_op jit(solution)/shard_map/reduce_scatter | solution.py:276
  487.7 320.2 %reduce-scatter.15.cloned.1.call-start = ((), (), s32[]{:S(2)}) async-start(), calls=%async_computation.13 | async-start | bytes 9732096 | tf_op jit(solution)/shard_map/reduce_scatter | solution.py:280
  495.1 454.4 %reduce-scatter.17.cloned.1.call-start = ((), (), s32[]{:S(2)}) async-start(), calls=%async_computation.14 | async-start | bytes 9732096 | tf_op jit(solution)/shard_map/reduce_scatter | solution.py:282
  504.4 56.2 %copy-start.42 = (bf16[1,512,768]{2,1,0:T(8,128)(2,1)S(1)}, bf16[1,512,768]{2,1,0:T(8,128)(2,1)}, u32[]{:S(2)}) copy-start(bf16[1,512,768]{2,1,0:T(8,128)(2,1)} %param.19) | copy-start | bytes 2359300
  504.4 569.8 %reduce-scatter.19.cloned.1.call-start = ((), (), s32[]{:S(2)}) async-start(), calls=%async_computation.17 | async-start | bytes 7299072
  574.9 48.0 %copy-start.15 = (f32[512,768]{1,0:T(8,128)S(1)}, f32[512,768]{1,0:T(8,128)}, u32[]{:S(2)}) copy-start(f32[512,768]{1,0:T(8,128)} %copy-done.14) | copy-start | bytes 4718596
  574.9 47.9 %copy-start.35 = (f32[512]{0:T(512)S(1)}, f32[512]{0:T(512)}, u32[]{:S(2)}) copy-start(f32[512]{0:T(512)} %copy-done.34) | copy-start | bytes 6148
  (66 other events, 215.2 us)
Sparse Core Ops, SparseCore 0:
  10.9 62.7 all-gather.8
  81.5 27.2 all-gather.16
  111.0 28.4 all-gather.18
  142.3 53.9 all-gather.10
  199.1 62.4 all-gather.12
  264.3 61.8 all-gather.14
  484.2 36.0 reduce-scatter.8
  522.8 37.7 reduce-scatter.10
  566.4 99.7 reduce-scatter.12
  672.5 135.2 reduce-scatter.14
  814.3 135.1 reduce-scatter.16
  955.6 118.5 reduce-scatter.18
where the time goes:
time: 1090 us; the launch traced here: 1080 us
  waiting for transfers between devices  641 us (59%)
  matrix products  208 us (19%)
  local copies, waits for them, and re-layouts  85 us (8%)
  blocking collectives  82.7 us (8%)
  other arithmetic  42.1 us (4%)
  between operations  15 us (1%)
    reduce_scatter x1, waiting for transfers between devices, shards(): lax.psum_scatter(down_weight_grad, ('dp', 'ctx'), scatter_dimension=0, ti...  142 us
    reduce_scatter x1, waiting for transfers between devices, shards(): lax.psum_scatter(up_weight_grad, ('dp', 'ctx'), scatter_dimension=0, tile...  142 us
    unnamed x13, waiting for transfers between devices  128 us
    unnamed x2, blocking collectives  82.7 us
    all_gather x1, waiting for transfers between devices, shards(): lax.all_gather(down_weight, ('dp', 'ctx'), axis=0, tiled=True)  43.6 us
    reduce_scatter x1, waiting for transfers between devices, shards(): lax.psum_scatter(grad_values.astype(jnp.bfloat16), 'ctx', scatter_dimensi...  40.3 us
    dot_general x8, matrix products, block_pieces(): jnp.einsum('bqhd,bkhd->bqhk', queries, block_keys, preferred_element_type...  38.8 us
    reduce_scatter x1, waiting for transfers between devices, shards(): lax.psum_scatter(output_weight_grad, ('dp', 'ctx'), scatter_dimension=0,...  37.6 us
  transfers between devices with their start and end apart: 12, of which 11 were waited for; matrix products, arithmetic and copies ran while one was open for 15% of the time, Pallas kernels for 0%

commit v1 on v0

--- a/solution.py
+++ b/solution.py
@@ -118,8 +118,11 @@
         jnp.zeros((seq_count, group, HEADS), jnp.float32),
         jnp.zeros((seq_count, group, HEADS), jnp.float32),
     )
-    piece_keys = lax.all_gather(key_rows, "ctx", axis=1, tiled=True)
-    piece_values = lax.all_gather(value_rows, "ctx", axis=1, tiled=True)
+    piece_keys, piece_values = jnp.split(
+        lax.all_gather(jnp.concatenate([key_rows, value_rows], axis=0), "ctx", axis=1, tiled=True),
+        [key_rows.shape[0]],
+        axis=0,
+    )
     span = piece_keys.shape[1]
     block_size = 512
 

time: 1090 us -> 1120 us (1.028)
  matrix products: 208 us -> 251 us
    dot_general x4, matrix products: 12.4 us -> 36.4 us  [forward_one_block(): jnp.einsum('bqhk,bkhd->bqhd', weights.astype(jnp.bfloat16), block_values,...]
    all_gather x1, waiting for transfers between devices: 28.9 us -> 7.64 us  [shards(): lax.all_gather(up_weight, ('dp', 'ctx'), axis=0, tiled=True)]
    all_gather x2 -> x3, waiting for transfers between devices: 48.2 us -> 67.7 us  [the longest x1 40.5 us: shards(): lax.all_gather(jnp.concatenate([key_rows, value_rows], axis=0), 'ctx', ax...]
    dot_general x8, matrix products: 38.8 us -> 51.4 us  [block_pieces(): jnp.einsum('bqhd,bkhd->bqhk', queries, block_keys, preferred_element_type...]
    dot_general x4, matrix products: 19.9 us -> 31.2 us  [backward_one_block(): jnp.einsum('bqhk,bqhd->bkhd', probs.astype(jnp.bfloat16), grad_mixed, pre...]
    unnamed x103 -> x99, local copies, waits for them, and re-layouts: 35.2 us -> 24.9 us
    unnamed x13 -> x14, waiting for transfers between devices: 128 us -> 129 us
  transfers between devices with their start and end apart: 12 -> 13, of which waited for: 11 -> 11; matrix products, arithmetic and copies ran while one was open for 15% -> 19% of each run, Pallas kernels for 0% -> 0%
where the time goes in v1:
time: 1120 us
  waiting for transfers between devices  642 us (57%)
  matrix products  251 us (22%)
  blocking collectives  82.7 us (7%)
  local copies, waits for them, and re-layouts  78.2 us (7%)
  other arithmetic  43.1 us (4%)
  between operations  14.8 us (1%)
    reduce_scatter x1, waiting for transfers between devices, shards(): lax.psum_scatter(up_weight_grad, ('dp', 'ctx'), scatter_dimension=0, tile...  142 us
    reduce_scatter x1, waiting for transfers between devices, shards(): lax.psum_scatter(down_weight_grad, ('dp', 'ctx'), scatter_dimension=0, ti...  141 us
    unnamed x14, waiting for transfers between devices  129 us
    unnamed x2, blocking collectives  82.7 us
    dot_general x8, matrix products, block_pieces(): jnp.einsum('bqhd,bkhd->bqhk', queries, block_keys, preferred_element_type...  51.4 us
    all_gather x1, waiting for transfers between devices, shards(): lax.all_gather(down_weight, ('dp', 'ctx'), axis=0, tiled=True)  44.6 us
    all_gather x1, waiting for transfers between devices, shards(): lax.all_gather(jnp.concatenate([key_rows, value_rows], axis=0), 'ctx', ax...  40.5 us
    reduce_scatter x1, waiting for transfers between devices, shards(): lax.psum_scatter(grad_values.astype(jnp.bfloat16), 'ctx', scatter_dimensi...  40.3 us
  transfers between devices with their start and end apart: 13, of which 11 were waited for; matrix products, arithmetic and copies ran while one was open for 19% of the time, Pallas kernels for 0%

profile of v1, /device:TPU:0, one launch (start us, length us, event | category | flops | bytes accessed | tf_op | source)
XLA Modules:
  0.0 1118.6 jit_solution(4512615820760395736)
XLA Ops:
  14.7 42.5 %all-reduce.17 = (bf16[1536]{0:T(1024)(128)(2,1)S(1)}, bf16[768]{0:T(1024)(128)(2,1)S(1)}, bf16[768]{0:T(1024)(128)(2,1)S(1)}, bf16[768]{0:T(1024)(128)(2,1)S(1)...) all-reduce(bf16[1536]{0:T(1024)(128)(2,1)S(1)} %dynamic-update-slic, ...), channel_id=1, replica_groups=mesh['dp'=8,'ctx'=4] {'dp','ctx'}, use_global_device_ids=true, to_apply=%add | all-reduce | flops 9216 | bytes 36864
  57.3 16.5 %all-gather.10.cloned.1.call-done = bf16[768,2304]{1,0:T(8,128)(2,1)} async-done(((bf16[24,2304]{1,0:T(8,128)(2,1)}), bf16[768,2304]{1,0:T(8,128)(2,1)}) %all-gather.10.cloned.1.call-update) | async-done | bytes 3538960 | tf_op jit(solution)/shard_map/all_gather | solution.py:52
  87.6 40.5 %all-gather.12.cloned.1.call-done = bf16[2,2048,768]{2,1,0:T(8,128)(2,1)} async-done(((bf16[2,512,768]{2,1,0:T(8,128)(2,1)}), bf16[2,2048,768]{2,1,0:T(8,128)(2,1)}) %all-gather.12.cloned.1.call-update) | async-done | bytes 6291472 | tf_op jit(solution)/shard_map/all_gather | solution.py:122
  134.1 103.9 %while.30 = (s32[]{:T(128)}, f32[1,512,12,64]{1,3,2,0:T(8,128)}, f32[1,512,12]{1,2,0:T(8,128)S(1)}, f32[1,512,12]{1,2,0:T(8,128)S(1)}, s32[1,512]{1,0:T(1,128)S(...) while((s32[]{:T(128)}, f32[1,512,12,64]{1,3,2,0:T(8,128)}, ...), condition=%wide.region_3.4_spmd.clone, body=%wide.region_0.3_spmd.clone.sunk | while | flops 832213504 | bytes 50998480 | solution.py:145
  150.9 8.6 bitcast_add_fusion.6
  176.6 9.1 bitcast_add_fusion.6
  202.5 9.0 bitcast_add_fusion.6
  228.3 9.7 bitcast_add_fusion.6
  250.4 20.0 %multiply_convert_fusion = (bf16[512,3072]{1,0:T(8,128)(2,1)}, f32[512,3072]{1,0:T(8,128)}, f32[512,3072]{1,0:T(8,128)}) fusion(f32[3072]{0:T(1024)S(1)} %convert_element_type.115, bf16[768,3072]{1,0:T(8,128)(2,1)} %all-gather.16.cloned.1.call-done, f32[512,768]{1,0:T(8,128)S(1)} %get-tuple-element.445, f32[768]{0:T(1024)S(1)} %convert_element_type.113, ...), kind=kOutput, calls=%fused_computation.55 | convolution fusion | flops 2521694208 | bytes 22042624 | tf_op jit(solution)/shard_map/dot_general | solution.py:161
  270.4 44.6 %all-gather.18.cloned.1.call-done = bf16[3072,768]{1,0:T(8,128)(2,1)} async-done(((bf16[96,768]{1,0:T(8,128)(2,1)}), bf16[3072,768]{1,0:T(8,128)(2,1)}) %all-gather.18.cloned.1.call-update) | async-done | bytes 4718608 | tf_op jit(solution)/shard_map/all_gather | solution.py:60
  325.6 8.8 convert_reduce_fusion
  346.3 27.1 %all-gather.22.cloned.1.call-done = bf16[2048,768]{1,0:T(8,128)(2,1)} async-done(((bf16[512,768]{1,0:T(8,128)(2,1)}), bf16[2048,768]{1,0:T(8,128)(2,1)}) %all-gather.22.cloned.1.call-update) | async-done | bytes 3145744 | tf_op jit(solution)/shard_map/all_gather | solution.py:219
  377.5 142.6 %while.31 = (s32[]{:T(128)}, f32[1,512,12,64]{1,3,2,0:T(8,128)}, bf16[1,2048,768]{1,2,0:T(8,128)(2,1)}, bf16[1,2048,768]{1,2,0:T(8,128)(2,1)}, s32[4]{0:T(128)S(...) while((s32[]{:T(128)}, f32[1,512,12,64]{1,3,2,0:T(8,128)}, ...), condition=%wide.region_14.15_spmd.clone, body=%wide.region_13.14_spmd.clone.sunk | while | flops 2046034432 | bytes 114953560 | solution.py:250
  398.3 7.8 fusion.132
  469.5 7.8 fusion.132
  532.2 8.2 fusion.67
  542.0 16.0 %reduce-scatter.9.cloned.1.call-done = bf16[1,512,768]{1,2,0:T(8,128)(2,1)} async-done(((bf16[1,2048,768]{1,2,0:T(8,128)(2,1)}), bf16[1,512,768]{1,2,0:T(8,128)(2,1)}) %reduce-scatter.9.cloned.1.call-update) | async-done | bytes 786448 | tf_op jit(solution)/shard_map/reduce_scatter | solution.py:255
  558.0 40.3 %reduce-scatter.11.cloned.1.call-done = bf16[1,512,768]{1,2,0:T(8,128)(2,1)} async-done(((bf16[1,2048,768]{1,2,0:T(8,128)(2,1)}), bf16[1,512,768]{1,2,0:T(8,128)(2,1)}) %reduce-scatter.11.cloned.1.call-update) | async-done | bytes 786448 | tf_op jit(solution)/shard_map/reduce_scatter | solution.py:258
  604.5 8.0 copy.68
  615.7 40.2 %all-reduce.16 = (f32[1536]{0:T(1024)S(1)}, f32[768]{0:T(1024)S(1)}, f32[768]{0:T(1024)S(1)}, f32[768]{0:T(1024)S(1)}, f32[3072]{0:T(1024)S(1)}, /*index=5*/f32[...) all-reduce(f32[1536]{0:T(1024)S(1)} %pad_maximum_fusion.3, ...), channel_id=7, replica_groups=mesh['dp'=8,'ctx'=4] {'dp','ctx'}, use_global_device_ids=true, to_apply=%region_19.20.clone | all-reduce | flops 9216 | bytes 73728
  666.4 37.5 %reduce-scatter.13.cloned.1.call-done = f32[24,768]{1,0:T(8,128)} async-done(((f32[768,768]{1,0:T(8,128)}), f32[24,768]{1,0:T(8,128)}) %reduce-scatter.13.cloned.1.call-update) | async-done | bytes 73744 | tf_op jit(solution)/shard_map/reduce_scatter | solution.py:279
  703.9 141.7 %reduce-scatter.15.cloned.1.call-done = f32[24,3072]{1,0:T(8,128)} async-done(((f32[768,3072]{1,0:T(8,128)}), f32[24,3072]{1,0:T(8,128)}) %reduce-scatter.15.cloned.1.call-update) | async-done | bytes 294928 | tf_op jit(solution)/shard_map/reduce_scatter | solution.py:283
  845.6 141.5 %reduce-scatter.17.cloned.1.call-done = f32[96,768]{1,0:T(8,128)} async-done(((f32[3072,768]{1,0:T(8,128)}), f32[96,768]{1,0:T(8,128)}) %reduce-scatter.17.cloned.1.call-update) | async-done | bytes 294928 | tf_op jit(solution)/shard_map/reduce_scatter | solution.py:285
  987.1 124.8 %reduce-scatter.19.cloned.1.call-done = f32[24,2304]{1,0:T(8,128)} async-done(((f32[768,2304]{1,0:T(8,128)}), f32[24,2304]{1,0:T(8,128)}) %reduce-scatter.19.cloned.1.call-update) | async-done | bytes 221200
  (312 shorter events, 287.7 us)
Async XLA Ops:
  7.2 66.6 %all-gather.10.cloned.1.call-start = ((), (), s32[]{:S(2)}) async-start(), calls=%async_computation.6 | async-start | bytes 3649536 | tf_op jit(solution)/shard_map/all_gather | solution.py:52
  7.9 120.3 %all-gather.12.cloned.1.call-start = ((), (), s32[]{:S(2)}) async-start(), calls=%async_computation.7 | async-start | bytes 7864320 | tf_op jit(solution)/shard_map/all_gather | solution.py:122
  82.9 156.8 %all-gather.14.cloned.1.call-start = ((), (), s32[]{:S(2)}) async-start(), calls=%async_computation.8 | async-start | bytes 1216512 | tf_op jit(solution)/shard_map/all_gather | solution.py:54
  83.6 166.8 %all-gather.16.cloned.1.call-start = ((), (), s32[]{:S(2)}) async-start(), calls=%async_computation.9 | async-start | bytes 4866048 | tf_op jit(solution)/shard_map/all_gather | solution.py:58
  84.2 230.8 %all-gather.18.cloned.1.call-start = ((), (), s32[]{:S(2)}) async-start(), calls=%async_computation.10 | async-start | bytes 4866048 | tf_op jit(solution)/shard_map/all_gather | solution.py:60
  84.8 261.5 %all-gather.20.cloned.1.call-start = ((), (), s32[]{:S(2)}) async-start(), calls=%async_computation.16 | async-start | bytes 3932160 | tf_op jit(solution)/shard_map/all_gather | solution.py:218
  85.3 288.0 %all-gather.22.cloned.1.call-start = ((), (), s32[]{:S(2)}) async-start(), calls=%async_computation.17 | async-start | bytes 3932160 | tf_op jit(solution)/shard_map/all_gather | solution.py:219
  85.5 252.6 %copy-start.23 = (f32[768]{0:T(1024)}, f32[768]{0:T(1024)S(1)}, u32[]{:S(2)}) copy-start(f32[768]{0:T(1024)S(1)} %convert_element_type.112) | copy-start | bytes 9220
  85.5 229.5 %copy-start.30 = (f32[768]{0:T(1024)}, f32[768]{0:T(1024)S(1)}, u32[]{:S(2)}) copy-start(f32[768]{0:T(1024)S(1)} %convert_element_type.113) | copy-start | bytes 9220
  87.4 470.6 %reduce-scatter.9.cloned.1.call-start = ((), (), s32[]{:S(2)}) async-start(), calls=%async_computation.11 | async-start | bytes 3932160 | tf_op jit(solution)/shard_map/reduce_scatter | solution.py:255
  242.4 95.7 %copy-start.7 = (f32[512,768]{1,0:T(8,128)}, f32[512,768]{1,0:T(8,128)S(1)}, u32[]{:S(2)}) copy-start(f32[512,768]{1,0:T(8,128)S(1)} %get-tuple-element.445) | copy-start | bytes 4718596
  242.4 95.7 %copy-start.18 = (f32[512]{0:T(512)}, f32[512]{0:T(512)S(1)}, u32[]{:S(2)}) copy-start(f32[512]{0:T(512)S(1)} %broadcast_multiply_fusion.1) | copy-start | bytes 6148
  242.7 95.4 %copy-start.26 = (f32[512]{0:T(512)}, f32[512]{0:T(512)S(1)}, u32[]{:S(2)}) copy-start(f32[512]{0:T(512)S(1)} %fusion.50) | copy-start | bytes 6148
  324.4 10.0 slice-start
  325.2 9.2 copy-start.15
  325.6 8.8 slice-start.1
  520.1 78.2 %reduce-scatter.11.cloned.1.call-start = ((), (), s32[]{:S(2)}) async-start(), calls=%async_computation.12 | async-start | bytes 3932160 | tf_op jit(solution)/shard_map/reduce_scatter | solution.py:258
  520.9 182.9 %reduce-scatter.13.cloned.1.call-start = ((), (), s32[]{:S(2)}) async-start(), calls=%async_computation.13 | async-start | bytes 2433024 | tf_op jit(solution)/shard_map/reduce_scatter | solution.py:279
  523.7 321.9 %reduce-scatter.15.cloned.1.call-start = ((), (), s32[]{:S(2)}) async-start(), calls=%async_computation.14 | async-start | bytes 9732096 | tf_op jit(solution)/shard_map/reduce_scatter | solution.py:283
  531.1 455.9 %reduce-scatter.17.cloned.1.call-start = ((), (), s32[]{:S(2)}) async-start(), calls=%async_computation.15 | async-start | bytes 9732096 | tf_op jit(solution)/shard_map/reduce_scatter | solution.py:285
  540.4 57.9 %copy-start.36 = (bf16[1,512,768]{2,1,0:T(8,128)(2,1)S(1)}, bf16[1,512,768]{2,1,0:T(8,128)(2,1)}, u32[]{:S(2)}) copy-start(bf16[1,512,768]{2,1,0:T(8,128)(2,1)} %param.19) | copy-start | bytes 2359300
  540.5 571.4 %reduce-scatter.19.cloned.1.call-start = ((), (), s32[]{:S(2)}) async-start(), calls=%async_computation.18 | async-start | bytes 7299072
  612.6 47.9 %copy-start.10 = (f32[512,768]{1,0:T(8,128)S(1)}, f32[512,768]{1,0:T(8,128)}, u32[]{:S(2)}) copy-start(f32[512,768]{1,0:T(8,128)} %copy-done.9) | copy-start | bytes 4718596
  612.7 47.9 %copy-start.29 = (f32[512]{0:T(512)S(1)}, f32[512]{0:T(512)}, u32[]{:S(2)}) copy-start(f32[512]{0:T(512)} %copy-done.28) | copy-start | bytes 6148
  (38 other events, 101.2 us)
Sparse Core Ops, SparseCore 0:
  10.9 62.7 all-gather.9
  83.0 45.1 all-gather.11
  131.1 53.9 all-gather.13
  187.9 62.4 all-gather.15
  253.1 61.8 all-gather.17
  316.4 26.8 all-gather.19
  344.8 28.4 all-gather.21
  520.2 37.7 reduce-scatter.8
  560.5 37.7 reduce-scatter.10
  604.0 99.8 reduce-scatter.12
  710.3 135.2 reduce-scatter.14
  851.9 135.0 reduce-scatter.16
  993.3 118.5 reduce-scatter.18
